TPU v7x, 256 devices: a whole 4x4x8 slice. The times are simulated.
256 devices in a mesh: dp: 8 (over z_lo, core), mp: 16 (over x, y), group: 2 (over z_hi).
Axes of the slice: x: 4, y: 4, z: 8 (z_hi: 2, z_lo: 4; z = z_hi * 4 + z_lo), core: 2. Of those that a mesh axis runs over, the one named last changes fastest.
Arguments:
- hidden: bfloat16 [1024, 8192], P('dp', 'mp'), may hold values from -6 to 6
- neighbour_ids: int32 [16, 2, 128], P('dp', 'group'), may hold values from 0 to 65535, as said below
- counts: int32 [16], P('dp'), may hold values from 0 to 2
- embed_table: bfloat16 [65536, 8192], P(('dp', 'group'), 'mp'), may hold values from -6 to 6
- w_query: bfloat16 [8192, 4096], P('group', 'mp'), may hold values from -0.0625 to 0.0625
- w_key: bfloat16 [8192, 4096], P('group', 'mp'), may hold values from -0.0625 to 0.0625
- w_value: bfloat16 [8192, 4096], P('group', 'mp'), may hold values from -0.0625 to 0.0625
- w_out: bfloat16 [4096, 8192], P('mp', 'group'), may hold values from -0.09375 to 0.09375
- grad_out: bfloat16 [1024, 8192], P('dp', 'mp'), may hold values from -6 to 6
Outputs:
- output: float32 [1024, 8192], P('dp', 'mp')
- grad_hidden: float32 [1024, 8192], P('dp', 'mp')
- grad_neighbours: float32 [16, 2, 128, 8192], P('dp', 'group', None, 'mp')
Inputs may be any that keep to these rules, and one draw needn't show every extreme that they name: `neighbour_ids`: token ids of the retrieved neighbours; the ids are split into 16 owners of 4096 consecutive ids each; of the 256 ids of one window's neighbour k (blocks of one window, one k), at most 64 belong to one owner, and exactly 64 belong to some owner. neighbours k < counts[c] of block c are used, the others are masked.
All inputs are finite; a program needn't handle non-finite values.
Results may differ from a plain program's by a relative error of at most 0.019.
Values may be sent and summed in bfloat16 or wider, within the bound.
A program may use at most 128 MiB of HBM per device.

v0:
```python
import math
import jax
import jax.numpy as jnp
from jax import lax
from jax.sharding import PartitionSpec as P

HD = 128
BLOCK = 64
RET = 128


def contract(left, right):
    return lax.dot_general(
        left, right, (((1,), (1,)), ((), ())), preferred_element_type=jnp.float32
    )


def per_device(
    hidden, neighbour_ids, counts, embed_table, w_query, w_key, w_value, w_out, grad_out
):
    tail_rows = BLOCK - 1
    rows_here = hidden.shape[0]
    blocks_here = rows_here // BLOCK
    heads_here = w_query.shape[1] // HD
    inv_root = 1.0 / math.sqrt(HD)
    keep_rows = rows_here - tail_rows
    pad_rows = jnp.zeros((tail_rows, hidden.shape[1]), jnp.bfloat16)
    query_rows = jnp.concatenate([hidden[tail_rows:], pad_rows], 0)
    grad_rows = jnp.concatenate([grad_out[tail_rows:], pad_rows], 0)
    full_query, full_grad = (
        lax.all_gather(query_rows, "mp", axis=1, tiled=True),
        lax.all_gather(grad_rows, "mp", axis=1, tiled=True),
    )
    flat_ids = neighbour_ids.reshape(-1)
    block_rows = embed_table.shape[0]
    owners = lax.axis_size("dp") * lax.axis_size("group")
    cap = flat_ids.shape[0] // 4
    every_id = (
        lax.all_gather(flat_ids.astype(jnp.float32), ("dp", "group"), axis=0, tiled=True)
        .astype(jnp.int32)
        .reshape(owners, -1)
    )
    owner = lax.axis_index("dp") * lax.axis_size("group") + lax.axis_index("group")
    local_ids = every_id - owner * block_rows
    inside = (local_ids >= 0) & (local_ids < block_rows)
    rank = jnp.cumsum(inside.astype(jnp.int32), axis=1) - 1
    slot_hit = inside[:, :, None] & (rank[:, :, None] == jnp.arange(cap)[None, None, :])
    send_rows = jnp.sum(jnp.where(slot_hit, local_ids[:, :, None], 0), axis=1)
    send_buf = embed_table[send_rows.reshape(-1)].reshape(owners, cap, -1)
    recv_buf = lax.all_to_all(send_buf, ("dp", "group"), 0, 0, tiled=True)
    own_owner = flat_ids // block_rows
    same_owner = own_owner[:, None] == jnp.arange(owners)[None, :]
    own_rank = (
        jnp.sum(jnp.where(same_owner, jnp.cumsum(same_owner.astype(jnp.int32), axis=0), 0), axis=1)
        - 1
    )
    own_cols = recv_buf.reshape(owners * cap, -1)[own_owner * cap + own_rank]
    neighbours = lax.all_gather(own_cols, "mp", axis=1, tiled=True)
    wq_full, wk_full, wv_full = (
        lax.all_gather(w_query, "group", axis=0, tiled=True),
        lax.all_gather(w_key, "group", axis=0, tiled=True),
        lax.all_gather(w_value, "group", axis=0, tiled=True),
    )
    query_sum = jnp.dot(full_query, wq_full, preferred_element_type=jnp.float32)
    query = query_sum.astype(jnp.bfloat16)
    wo_full = lax.all_gather(w_out, "group", axis=1, tiled=True)
    keys = jnp.dot(neighbours, wk_full, preferred_element_type=jnp.float32).astype(jnp.bfloat16)
    values = jnp.dot(neighbours, wv_full, preferred_element_type=jnp.float32).astype(jnp.bfloat16)
    key_block = keys.reshape(blocks_here, RET, heads_here, HD)
    value_block = values.reshape(blocks_here, RET, heads_here, HD)
    query_block = query.reshape(blocks_here, BLOCK, heads_here, HD)
    live = (counts > lax.axis_index("group")).astype(jnp.float32)
    scores = (
        jnp.einsum("cqhd,ckhd->chqk", query_block, key_block, preferred_element_type=jnp.float32)
        * inv_root
    )
    weights = jnp.exp(scores) * live[:, None, None, None]
    numer = jnp.einsum(
        "chqk,ckhd->cqhd",
        weights.astype(jnp.bfloat16),
        value_block,
        preferred_element_type=jnp.float32,
    )
    partial_total = jnp.sum(weights, -1)
    numer, partial_total = lax.psum((numer, partial_total), "group")
    total = partial_total + 1.0
    attn = numer / jnp.transpose(total, (0, 2, 1))[..., None]
    attn_bf = attn.reshape(rows_here, heads_here * HD).astype(jnp.bfloat16)
    out_term = jnp.dot(attn_bf, wo_full, preferred_element_type=jnp.float32)
    d_attn = contract(full_grad, wo_full).astype(jnp.bfloat16)
    d_block = d_attn.reshape(blocks_here, BLOCK, heads_here, HD)
    prob = weights / total[..., None]
    d_prob = jnp.einsum("cqhd,ckhd->chqk", d_block, value_block, preferred_element_type=jnp.float32)
    delta = jnp.sum(d_block.astype(jnp.float32) * attn, -1)
    d_score = (prob * (d_prob - jnp.transpose(delta, (0, 2, 1))[..., None])).astype(jnp.bfloat16)
    query_part = jnp.einsum(
        "chqk,ckhd->cqhd", d_score, key_block, preferred_element_type=jnp.float32
    )
    query_grad = lax.psum(query_part, "group")
    d_query = (query_grad * inv_root).astype(jnp.bfloat16).reshape(rows_here, heads_here * HD)
    d_keys = (
        jnp.einsum("chqk,cqhd->ckhd", d_score, query_block, preferred_element_type=jnp.float32)
        * inv_root
    ).astype(jnp.bfloat16)
    d_values = jnp.einsum(
        "chqk,cqhd->ckhd", prob.astype(jnp.bfloat16), d_block, preferred_element_type=jnp.float32
    ).astype(jnp.bfloat16)
    d_keys = d_keys.reshape(blocks_here * RET, heads_here * HD)
    d_values = d_values.reshape(blocks_here * RET, heads_here * HD)
    hid_term = contract(d_query, wq_full)
    out_cols, hid_cols = (
        lax.psum_scatter(
            out_term.astype(jnp.bfloat16), "mp", scatter_dimension=1, tiled=True
        ).astype(jnp.float32),
        lax.psum_scatter(
            hid_term.astype(jnp.bfloat16), "mp", scatter_dimension=1, tiled=True
        ).astype(jnp.float32),
    )
    zero_rows = jnp.zeros((tail_rows, out_cols.shape[1]), jnp.float32)
    output = jnp.concatenate([zero_rows, out_cols[:keep_rows]], 0)
    grad_hidden = jnp.concatenate([zero_rows, hid_cols[:keep_rows]], 0)
    neigh_term = contract(d_keys, wk_full) + contract(d_values, wv_full)
    neigh_cols = lax.psum_scatter(
        neigh_term.astype(jnp.bfloat16), "mp", scatter_dimension=1, tiled=True
    ).astype(jnp.float32)
    grad_neighbours = neigh_cols.reshape(blocks_here, 1, RET, neigh_cols.shape[1])
    return (output, grad_hidden, grad_neighbours)


def solution(mesh):
    return jax.shard_map(
        per_device,
        mesh=mesh,
        in_specs=(
            P("dp", "mp"),
            P("dp", "group", None),
            P("dp"),
            P(("dp", "group"), "mp"),
            P("group", "mp"),
            P("group", "mp"),
            P("group", "mp"),
            P("mp", "group"),
            P("dp", "mp"),
        ),
        out_specs=(P("dp", "mp"), P("dp", "mp"), P("dp", "group", None, "mp")),
        check_vma=False,
    )
```

profile of v0, /device:TPU:2, one launch (start us, length us, event | category | flops | bytes accessed | tf_op | source)
XLA Modules:
  0.0 972.8 jit_solution(12286093274936307989)
XLA Ops:
  12.4 40.9 %all-gather.1 = f32[16,1,256]{2,1,0:T(1,128)S(1)} all-gather(f32[1,1,256]{2,1,0:T(1,128)S(1)} %bitcast.107), channel_id=1, replica_groups=mesh['dp'=8,'mp'=16,'group'=2] {'dp','group'}, dimensions={0}, use_global_device_ids=true | all-gather | bytes 17408 | tf_op jit(solution)/shard_map/all_gather | solution.py:39
  54.8 7.9 gather_fusion
  62.7 6.0 all-to-all-start
  69.8 38.2 %all-to-all-done = bf16[16,64,512]{2,1,0:T(8,128)(2,1)S(1)} async-done(((bf16[16,64,512]{2,1,0:T(8,128)(2,1)}), bf16[16,64,512]{2,1,0:T(8,128)(2,1)S(1)}, u32[]{:S(2)}, u32[]{:S(2)}) %all-to-all-start) | async-done | bytes 1048608 | tf_op jit(solution)/shard_map/all_to_all | solution.py:50
  110.7 60.2 %all-gather.14.cloned.1.call-done = bf16[8192,256]{1,0:T(8,128)(2,1)} async-done(((bf16[4096,256]{1,0:T(8,128)(2,1)}), bf16[8192,256]{1,0:T(8,128)(2,1)}) %all-gather.14.cloned.1.call-update) | async-done | bytes 4194320 | tf_op jit(solution)/shard_map/all_gather | solution.py:60
  170.9 3.5 convolution_convert_fusion.6
  174.4 65.6 %all-gather.20.cloned.1.call-done = bf16[128,8192]{1,0:T(8,128)(2,1)} async-done(((bf16[128,512]{1,0:T(8,128)(2,1)}), bf16[128,8192]{1,0:T(8,128)(2,1)}) %all-gather.20.cloned.1.call-update) | async-done | bytes 2097168 | tf_op jit(solution)/shard_map/all_gather | solution.py:32
  240.0 113.4 %all-gather.18.cloned.1.call-done = bf16[256,8192]{1,0:T(8,128)(2,1)} async-done(((bf16[256,4096]{1,0:T(8,128)(2,1)}), bf16[256,8192]{1,0:T(8,128)(2,1)}) %all-gather.18.cloned.1.call-update) | async-done | bytes 4194320 | tf_op jit(solution)/shard_map/all_gather | solution.py:66
  353.4 4.4 convolution_convert_fusion.5
  357.8 105.4 %all-gather.10.cloned.1.call-done = bf16[8192,256]{1,0:T(8,128)(2,1)} async-done(((bf16[4096,256]{1,0:T(8,128)(2,1)}), bf16[8192,256]{1,0:T(8,128)(2,1)}) %all-gather.10.cloned.1.call-update) | async-done | bytes 4194320 | tf_op jit(solution)/shard_map/all_gather | solution.py:62
  463.2 61.3 %all-gather.22.cloned.1.call-done = bf16[256,8192]{1,0:T(8,128)(2,1)} async-done(((bf16[256,512]{1,0:T(8,128)(2,1)}), bf16[256,8192]{1,0:T(8,128)(2,1)}) %all-gather.22.cloned.1.call-update) | async-done | bytes 4194320 | tf_op jit(solution)/shard_map/all_gather | solution.py:58
  524.5 4.7 convolution_convert_fusion.4
  529.2 108.8 %all-gather.16.cloned.1.call-done = bf16[8192,256]{1,0:T(8,128)(2,1)} async-done(((bf16[4096,256]{1,0:T(8,128)(2,1)}), bf16[8192,256]{1,0:T(8,128)(2,1)}) %all-gather.16.cloned.1.call-update) | async-done | bytes 4194320 | tf_op jit(solution)/shard_map/all_gather | solution.py:61
  638.1 4.7 convolution_convert_fusion.3
  644.0 8.8 psum.22
  652.9 25.8 %all-reduce.7.cloned.1.call-done = f32[2,64,2,128]{3,1,2,0:T(8,128)} async-done(((f32[2,64,2,128]{3,1,2,0:T(8,128)}), f32[2,64,2,128]{3,1,2,0:T(8,128)}) %all-reduce.7.cloned.1.call-update) | async-done | bytes 131088 | tf_op jit(solution)/shard_map/psum | solution.py:85
  681.0 4.3 convolution_convert_fusion.1
  685.3 31.5 %all-reduce.9.cloned.1.call-done = f32[2,64,2,128]{3,1,2,0:T(8,128)} async-done(((f32[2,64,2,128]{3,1,2,0:T(8,128)}), f32[2,64,2,128]{3,1,2,0:T(8,128)}) %all-reduce.9.cloned.1.call-update) | async-done | bytes 131088 | tf_op jit(solution)/shard_map/psum | solution.py:99
  717.9 5.0 convolution_convert_fusion
  724.0 3.6 fusion.11
  727.6 3.2 fusion
  730.8 64.9 %reduce-scatter.4.cloned.1.call-done = bf16[128,512]{1,0:T(8,128)(2,1)} async-done(((bf16[128,8192]{1,0:T(8,128)(2,1)}), bf16[128,512]{1,0:T(8,128)(2,1)}) %reduce-scatter.4.cloned.1.call-update) | async-done | bytes 131088 | tf_op jit(solution)/shard_map/reduce_scatter | solution.py:112
  797.3 81.1 %reduce-scatter.6.cloned.1.call-done = bf16[128,512]{1,0:T(8,128)(2,1)} async-done(((bf16[128,8192]{1,0:T(8,128)(2,1)}), bf16[128,512]{1,0:T(8,128)(2,1)}) %reduce-scatter.6.cloned.1.call-update) | async-done | bytes 131088 | tf_op jit(solution)/shard_map/reduce_scatter | solution.py:115
  880.1 84.0 %reduce-scatter.8.cloned.1.call-done = bf16[256,512]{1,0:T(8,128)(2,1)} async-done(((bf16[256,8192]{1,0:T(8,128)(2,1)}), bf16[256,512]{1,0:T(8,128)(2,1)}) %reduce-scatter.8.cloned.1.call-update) | async-done | bytes 262160 | tf_op jit(solution)/shard_map/reduce_scatter | solution.py:123
  (86 shorter events, 20.9 us)
Async XLA Ops:
  7.2 5.2 copy-start.1
  7.2 103.5 %all-gather.12.cloned.1.call-start = ((), (), s32[]{:S(2)}) async-start(), calls=%async_computation.5 | async-start | bytes 2228224 | tf_op jit(solution)/shard_map/all_gather | solution.py:31
  8.8 162.1 %all-gather.14.cloned.1.call-start = ((), (), s32[]{:S(2)}) async-start(), calls=%async_computation.6 | async-start | bytes 6291456 | tf_op jit(solution)/shard_map/all_gather | solution.py:60
  9.6 230.4 %all-gather.20.cloned.1.call-start = ((), (), s32[]{:S(2)}) async-start(), calls=%async_computation.11 | async-start | bytes 2228224 | tf_op jit(solution)/shard_map/all_gather | solution.py:32
  11.2 342.2 %all-gather.18.cloned.1.call-start = ((), (), s32[]{:S(2)}) async-start(), calls=%async_computation.9 | async-start | bytes 6291456 | tf_op jit(solution)/shard_map/all_gather | solution.py:66
  11.8 451.4 %all-gather.10.cloned.1.call-start = ((), (), s32[]{:S(2)}) async-start(), calls=%async_computation.4 | async-start | bytes 6291456 | tf_op jit(solution)/shard_map/all_gather | solution.py:62
  62.7 47.9 %copy-start.2 = (s32[2]{0:T(128)S(1)}, s32[2]{0:T(128)}, u32[]{:S(2)}) copy-start(s32[2]{0:T(128)} %param.11) | copy-start | bytes 28
  62.7 45.2 %all-to-all-start = ((bf16[16,64,512]{2,1,0:T(8,128)(2,1)}), bf16[16,64,512]{2,1,0:T(8,128)(2,1)S(1)}, u32[]{:S(2)}, u32[]{:S(2)}) async-start(bf16[16,64,512]{2,1,0:T(8,128)(2,1)} %bitcast.4), calls=%async_computation | async-start | bytes 2097152 | tf_op jit(solution)/shard_map/all_to_all | solution.py:50
  68.7 455.8 %all-gather.22.cloned.1.call-start = ((), (), s32[]{:S(2)}) async-start(), calls=%async_computation.15 | async-start | bytes 4456448 | tf_op jit(solution)/shard_map/all_gather | solution.py:58
  109.8 528.2 %all-gather.16.cloned.1.call-start = ((), (), s32[]{:S(2)}) async-start(), calls=%async_computation.7 | async-start | bytes 6291456 | tf_op jit(solution)/shard_map/all_gather | solution.py:61
  110.6 568.1 %all-reduce.7.cloned.1.call-start = ((), (), s32[]{:S(2)}) async-start(), calls=%async_computation.8 | async-start | bytes 262144 | tf_op jit(solution)/shard_map/psum | solution.py:85
  644.0 72.9 %all-reduce.9.cloned.1.call-start = ((), (), s32[]{:S(2)}) async-start(), calls=%async_computation.12 | async-start | bytes 262144 | tf_op jit(solution)/shard_map/psum | solution.py:99
  680.9 114.8 %reduce-scatter.4.cloned.1.call-start = ((), (), s32[]{:S(2)}) async-start(), calls=%async_computation.10 | async-start | bytes 2228224 | tf_op jit(solution)/shard_map/reduce_scatter | solution.py:112
  685.3 193.2 %reduce-scatter.6.cloned.1.call-start = ((), (), s32[]{:S(2)}) async-start(), calls=%async_computation.13 | async-start | bytes 2228224 | tf_op jit(solution)/shard_map/reduce_scatter | solution.py:115
  722.9 241.2 %reduce-scatter.8.cloned.1.call-start = ((), (), s32[]{:S(2)}) async-start(), calls=%async_computation.14 | async-start | bytes 4456448 | tf_op jit(solution)/shard_map/reduce_scatter | solution.py:123
  723.9 3.6 copy-start
Sparse Core Ops, SparseCore 0:
  11.0 55.3 all-gather.11
  68.1 102.6 all-gather.13
  173.9 66.1 all-gather.19
  241.7 111.7 all-gather.17
  355.1 108.0 all-gather.9
  466.1 58.3 all-gather.21
  526.3 111.7 all-gather.15
  644.1 34.5 all-reduce.6
  681.9 34.9 all-reduce.8
  720.3 75.4 reduce-scatter.3
  799.7 78.6 reduce-scatter.5
  881.9 82.1 reduce-scatter.7
where the time goes:
time: 973 us
  waiting for transfers between devices  843 us (87%)
  blocking collectives  49.7 us (5%)
  matrix products  36.1 us (4%)
  local copies, waits for them, and re-layouts  15.7 us (2%)
  between operations  14.5 us (1%)
    all_gather x1, waiting for transfers between devices, per_device(): wo_full = lax.all_gather(w_out, 'group', axis=1, tiled=True)  113 us
    all_gather x1, waiting for transfers between devices, per_device(): lax.all_gather(w_key, 'group', axis=0, tiled=True)  109 us
    all_gather x1, waiting for transfers between devices, per_device(): lax.all_gather(w_value, 'group', axis=0, tiled=True)  105 us
    reduce_scatter x1, waiting for transfers between devices, per_device(): lax.psum_scatter(neigh_term.astype(jnp.bfloat16), 'mp', scatter_dimension...  84 us
    reduce_scatter x1, waiting for transfers between devices, per_device(): lax.psum_scatter(hid_term.astype(jnp.bfloat16), 'mp', scatter_dimension=1...  81.1 us
    all_gather x1, waiting for transfers between devices, per_device(): lax.all_gather(grad_rows, 'mp', axis=1, tiled=True)  65.6 us
    reduce_scatter x1, waiting for transfers between devices, per_device(): lax.psum_scatter(out_term.astype(jnp.bfloat16), 'mp', scatter_dimension=1...  64.9 us
    all_gather x1, waiting for transfers between devices, per_device(): neighbours = lax.all_gather(own_cols, 'mp', axis=1, tiled=True)  61.3 us
  transfers between devices with their start and end apart: 13, of which 12 were waited for; matrix products, arithmetic and copies ran while one was open for 5% of the time, Pallas kernels for 0%

commit v1 on v0

--- a/solution.py
+++ b/solution.py
@@ -3,6 +3,7 @@
 import jax.numpy as jnp
 from jax import lax
 from jax.sharding import PartitionSpec as P
+from jax.lax import axis_index, ppermute, psum
 
 HD = 128
 BLOCK = 64
@@ -55,7 +56,21 @@
         - 1
     )
     own_cols = recv_buf.reshape(owners * cap, -1)[own_owner * cap + own_rank]
-    neighbours = lax.all_gather(own_cols, "mp", axis=1, tiled=True)
+
+    def review_the_plate(my_tile):
+        n_slots = psum(1, "mp")
+        t_next = [(rr - 1, rr) for rr in range(1, n_slots)] + [(n_slots - 1, 0)]
+        then = my_tile
+        windows = [then]
+        j = 0
+        while j < n_slots - 1:
+            then = ppermute(then, "mp", t_next)
+            windows += [then]
+            j += 1
+        latest = jnp.concatenate([*reversed(windows)], 1)
+        return jnp.roll(latest, (axis_index("mp") + 1) * then.shape[1], 1)
+
+    neighbours = review_the_plate(own_cols)
     wq_full, wk_full, wv_full = (
         lax.all_gather(w_query, "group", axis=0, tiled=True),
         lax.all_gather(w_key, "group", axis=0, tiled=True),

time: 973 us -> 919 us (0.945)
  waiting for transfers between devices: 843 us -> 757 us
  local copies, waits for them, and re-layouts: 15.7 us -> 45.3 us
    ppermute x0 -> x15, waiting for transfers between devices: none -> 130 us  [review_the_plate(): then = ppermute(then, 'mp', t_next)]
    all_gather x1, waiting for transfers between devices: 65.6 us -> 3.02 us  [per_device(): lax.all_gather(grad_rows, 'mp', axis=1, tiled=True)]
    all_gather x1 -> x0, waiting for transfers between devices: 61.3 us -> none  [per_device(): neighbours = lax.all_gather(own_cols, 'mp', axis=1, tiled=True)]
    all_gather x1, waiting for transfers between devices: 60.2 us -> 0.01 us  [per_device(): lax.all_gather(w_query, 'group', axis=0, tiled=True)]
    all_gather x1, waiting for transfers between devices: 109 us -> 75.1 us  [per_device(): lax.all_gather(w_key, 'group', axis=0, tiled=True)]
    unnamed x7 -> x40, local copies, waits for them, and re-layouts: 0.01 us -> 29 us
  transfers between devices with their start and end apart: 13 -> 27, of which waited for: 12 -> 24; matrix products, arithmetic and copies ran while one was open for 5% -> 9% of each run, Pallas kernels for 0% -> 0%
where the time goes in v1:
time: 919 us; the launch traced here: 918 us
  waiting for transfers between devices  757 us (82%)
  blocking collectives  49.7 us (5%)
  local copies, waits for them, and re-layouts  45.3 us (5%)
  matrix products  36.1 us (4%)
  between operations  14.2 us (2%)
    ppermute x15, waiting for transfers between devices, review_the_plate(): then = ppermute(then, 'mp', t_next)  130 us
    all_gather x1, waiting for transfers between devices, per_device(): wo_full = lax.all_gather(w_out, 'group', axis=1, tiled=True)  117 us
    all_gather x1, waiting for transfers between devices, per_device(): lax.all_gather(w_value, 'group', axis=0, tiled=True)  95.9 us
    reduce_scatter x1, waiting for transfers between devices, per_device(): lax.psum_scatter(neigh_term.astype(jnp.bfloat16), 'mp', scatter_dimension...  84.1 us
    reduce_scatter x1, waiting for transfers between devices, per_device(): lax.psum_scatter(hid_term.astype(jnp.bfloat16), 'mp', scatter_dimension=1...  81 us
    all_gather x1, waiting for transfers between devices, per_device(): lax.all_gather(w_key, 'group', axis=0, tiled=True)  75.1 us
    reduce_scatter x1, waiting for transfers between devices, per_device(): lax.psum_scatter(out_term.astype(jnp.bfloat16), 'mp', scatter_dimension=1...  65 us
    all_gather x1, blocking collectives, per_device(): lax.all_gather(flat_ids.astype(jnp.float32), ('dp', 'group'), axis=0, til...  40.9 us
  transfers between devices with their start and end apart: 27, of which 24 were waited for; matrix products, arithmetic and copies ran while one was open for 9% of the time, Pallas kernels for 0%

profile of v1, /device:TPU:2, one launch (start us, length us, event | category | flops | bytes accessed | tf_op | source)
XLA Modules:
  0.0 917.9 jit_solution(3645485150476098056)
XLA Ops:
  12.5 40.9 %all-gather = f32[16,1,256]{2,1,0:T(1,128)S(1)} all-gather(f32[1,1,256]{2,1,0:T(1,128)S(1)} %bitcast.105), channel_id=1, replica_groups=mesh['dp'=8,'mp'=16,'group'=2] {'dp','group'}, dimensions={0}, use_global_device_ids=true | all-gather | bytes 17408 | tf_op jit(solution)/shard_map/all_gather | solution.py:40
  70.3 37.5 %all-to-all-done = bf16[16,64,512]{2,1,0:T(8,128)(2,1)S(1)} async-done(((bf16[16,64,512]{2,1,0:T(8,128)(2,1)}), bf16[16,64,512]{2,1,0:T(8,128)(2,1)S(1)}, u32[]{:S(2)}, u32[]{:S(2)}) %all-to-all-start) | async-done | bytes 1048608 | tf_op jit(solution)/shard_map/all_to_all | solution.py:51
  117.5 8.5 collective-permute-done.1
  126.0 8.7 collective-permute-done.2
  134.7 9.4 %collective-permute-done.3 = bf16[256,512]{1,0:T(8,128)(2,1)S(1)} collective-permute-done((bf16[256,512]{1,0:T(8,128)(2,1)S(1)}, bf16[256,512]{1,0:T(8,128)(2,1)S(1)}, u32[]{:S(2)}, u32[]{:S(2)}) %collective-permute-start.3) | collective-permute-done | bytes 262176 | tf_op jit(solution)/shard_map/ppermute | solution.py:67
  144.1 10.1 %collective-permute-done.4 = bf16[256,512]{1,0:T(8,128)(2,1)S(1)} collective-permute-done((bf16[256,512]{1,0:T(8,128)(2,1)S(1)}, bf16[256,512]{1,0:T(8,128)(2,1)S(1)}, u32[]{:S(2)}, u32[]{:S(2)}) %collective-permute-start.4) | collective-permute-done | bytes 262176 | tf_op jit(solution)/shard_map/ppermute | solution.py:67
  154.2 11.0 %collective-permute-done.5 = bf16[256,512]{1,0:T(8,128)(2,1)S(1)} collective-permute-done((bf16[256,512]{1,0:T(8,128)(2,1)S(1)}, bf16[256,512]{1,0:T(8,128)(2,1)S(1)}, u32[]{:S(2)}, u32[]{:S(2)}) %collective-permute-start.5) | collective-permute-done | bytes 262176 | tf_op jit(solution)/shard_map/ppermute | solution.py:67
  165.2 10.9 %collective-permute-done.6 = bf16[256,512]{1,0:T(8,128)(2,1)S(1)} collective-permute-done((bf16[256,512]{1,0:T(8,128)(2,1)S(1)}, bf16[256,512]{1,0:T(8,128)(2,1)S(1)}, u32[]{:S(2)}, u32[]{:S(2)}) %collective-permute-start.6) | collective-permute-done | bytes 262176 | tf_op jit(solution)/shard_map/ppermute | solution.py:67
  176.0 10.1 %collective-permute-done.7 = bf16[256,512]{1,0:T(8,128)(2,1)S(1)} collective-permute-done((bf16[256,512]{1,0:T(8,128)(2,1)S(1)}, bf16[256,512]{1,0:T(8,128)(2,1)S(1)}, u32[]{:S(2)}, u32[]{:S(2)}) %collective-permute-start.7) | collective-permute-done | bytes 262176 | tf_op jit(solution)/shard_map/ppermute | solution.py:67
  186.1 9.2 %collective-permute-done.8 = bf16[256,512]{1,0:T(8,128)(2,1)S(1)} collective-permute-done((bf16[256,512]{1,0:T(8,128)(2,1)S(1)}, bf16[256,512]{1,0:T(8,128)(2,1)S(1)}, u32[]{:S(2)}, u32[]{:S(2)}) %collective-permute-start.8) | collective-permute-done | bytes 262176 | tf_op jit(solution)/shard_map/ppermute | solution.py:67
  195.4 8.5 collective-permute-done.9
  203.9 8.9 collective-permute-done.10
  212.8 8.9 collective-permute-done.11
  221.8 9.0 collective-permute-done.12
  234.4 9.6 %collective-permute-done.13 = bf16[256,512]{1,0:T(8,128)(2,1)} collective-permute-done((bf16[256,512]{1,0:T(8,128)(2,1)}, bf16[256,512]{1,0:T(8,128)(2,1)}, u32[]{:S(2)}, u32[]{:S(2)}) %collective-permute-start.13) | collective-permute-done | bytes 262176 | tf_op jit(solution)/shard_map/ppermute | solution.py:67
  247.0 117.2 %all-gather.16.cloned.1.call-done = bf16[256,8192]{1,0:T(8,128)(2,1)} async-done(((bf16[256,4096]{1,0:T(8,128)(2,1)}), bf16[256,8192]{1,0:T(8,128)(2,1)}) %all-gather.16.cloned.1.call-update) | async-done | bytes 4194320 | tf_op jit(solution)/shard_map/all_gather | solution.py:81
  398.9 75.1 %all-gather.14.cloned.1.call-done = bf16[8192,256]{1,0:T(8,128)(2,1)} async-done(((bf16[4096,256]{1,0:T(8,128)(2,1)}), bf16[8192,256]{1,0:T(8,128)(2,1)}) %all-gather.14.cloned.1.call-update) | async-done | bytes 4194320 | tf_op jit(solution)/shard_map/all_gather | solution.py:76
  479.0 8.8 psum.22
  487.9 95.9 %all-gather.8.cloned.1.call-done = bf16[8192,256]{1,0:T(8,128)(2,1)} async-done(((bf16[4096,256]{1,0:T(8,128)(2,1)}), bf16[8192,256]{1,0:T(8,128)(2,1)}) %all-gather.8.cloned.1.call-update) | async-done | bytes 4194320 | tf_op jit(solution)/shard_map/all_gather | solution.py:77
  589.4 34.7 %all-reduce.7.cloned.1.call-done = f32[2,64,2,128]{3,1,2,0:T(8,128)} async-done(((f32[2,64,2,128]{3,1,2,0:T(8,128)}), f32[2,64,2,128]{3,1,2,0:T(8,128)}) %all-reduce.7.cloned.1.call-update) | async-done | bytes 131088 | tf_op jit(solution)/shard_map/psum | solution.py:100
  630.7 31.5 %all-reduce.9.cloned.1.call-done = f32[2,64,2,128]{3,1,2,0:T(8,128)} async-done(((f32[2,64,2,128]{3,1,2,0:T(8,128)}), f32[2,64,2,128]{3,1,2,0:T(8,128)}) %all-reduce.9.cloned.1.call-update) | async-done | bytes 131088 | tf_op jit(solution)/shard_map/psum | solution.py:114
  676.3 65.0 %reduce-scatter.4.cloned.1.call-done = bf16[128,512]{1,0:T(8,128)(2,1)} async-done(((bf16[128,8192]{1,0:T(8,128)(2,1)}), bf16[128,512]{1,0:T(8,128)(2,1)}) %reduce-scatter.4.cloned.1.call-update) | async-done | bytes 131088 | tf_op jit(solution)/shard_map/reduce_scatter | solution.py:127
  742.9 81.0 %reduce-scatter.6.cloned.1.call-done = bf16[128,512]{1,0:T(8,128)(2,1)} async-done(((bf16[128,8192]{1,0:T(8,128)(2,1)}), bf16[128,512]{1,0:T(8,128)(2,1)}) %reduce-scatter.6.cloned.1.call-update) | async-done | bytes 131088 | tf_op jit(solution)/shard_map/reduce_scatter | solution.py:130
  825.5 84.1 %reduce-scatter.8.cloned.1.call-done = bf16[256,512]{1,0:T(8,128)(2,1)} async-done(((bf16[256,8192]{1,0:T(8,128)(2,1)}), bf16[256,512]{1,0:T(8,128)(2,1)}) %reduce-scatter.8.cloned.1.call-update) | async-done | bytes 262160 | tf_op jit(solution)/shard_map/reduce_scatter | solution.py:138
  (147 shorter events, 109.3 us)
Async XLA Ops:
  7.2 223.6 %all-gather.10.cloned.1.call-start = ((), (), s32[]{:S(2)}) async-start(), calls=%async_computation.5 | async-start | bytes 2228224 | tf_op jit(solution)/shard_map/all_gather | solution.py:32
  8.8 222.0 %all-gather.12.cloned.1.call-start = ((), (), s32[]{:S(2)}) async-start(), calls=%async_computation.6 | async-start | bytes 6291456 | tf_op jit(solution)/shard_map/all_gather | solution.py:75
  9.6 237.4 %all-gather.18.cloned.1.call-start = ((), (), s32[]{:S(2)}) async-start(), calls=%async_computation.11 | async-start | bytes 2228224 | tf_op jit(solution)/shard_map/all_gather | solution.py:33
  11.2 353.0 %all-gather.16.cloned.1.call-start = ((), (), s32[]{:S(2)}) async-start(), calls=%async_computation.9 | async-start | bytes 6291456 | tf_op jit(solution)/shard_map/all_gather | solution.py:81
  62.8 45.0 %all-to-all-start = ((bf16[16,64,512]{2,1,0:T(8,128)(2,1)}), bf16[16,64,512]{2,1,0:T(8,128)(2,1)S(1)}, u32[]{:S(2)}, u32[]{:S(2)}) async-start(bf16[16,64,512]{2,1,0:T(8,128)(2,1)} %bitcast.4), calls=%async_computation | async-start | bytes 2097152 | tf_op jit(solution)/shard_map/all_to_all | solution.py:51
  68.6 405.3 %all-gather.14.cloned.1.call-start = ((), (), s32[]{:S(2)}) async-start(), calls=%async_computation.7 | async-start | bytes 6291456 | tf_op jit(solution)/shard_map/all_gather | solution.py:76
  69.2 514.6 %all-gather.8.cloned.1.call-start = ((), (), s32[]{:S(2)}) async-start(), calls=%async_computation.4 | async-start | bytes 6291456 | tf_op jit(solution)/shard_map/all_gather | solution.py:77
  126.0 8.7 collective-permute-start.2
  134.7 9.4 %collective-permute-start.3 = (bf16[256,512]{1,0:T(8,128)(2,1)S(1)}, bf16[256,512]{1,0:T(8,128)(2,1)S(1)}, u32[]{:S(2)}, u32[]{:S(2)}) collective-permute-start(bf16[256,512]{1,0:T(8,128)(2,1)S(1)} %collective-permute-done.2), channel_id=1, source_target_pairs={{0,2},{2,4},{4,6},{6,8},{8,10},{10,12},{12,14},{14,16},{16,18},{18... | collective-permute-start | bytes 786440 | tf_op jit(solution)/shard_map/ppermute | solution.py:67
  144.1 10.1 %collective-permute-start.4 = (bf16[256,512]{1,0:T(8,128)(2,1)S(1)}, bf16[256,512]{1,0:T(8,128)(2,1)S(1)}, u32[]{:S(2)}, u32[]{:S(2)}) collective-permute-start(bf16[256,512]{1,0:T(8,128)(2,1)S(1)} %collective-permute-done.3), channel_id=1, source_target_pairs={{0,2},{2,4},{4,6},{6,8},{8,10},{10,12},{12,14},{14,16},{16,18},{18... | collective-permute-start | bytes 786440 | tf_op jit(solution)/shard_map/ppermute | solution.py:67
  154.2 11.0 %collective-permute-start.5 = (bf16[256,512]{1,0:T(8,128)(2,1)S(1)}, bf16[256,512]{1,0:T(8,128)(2,1)S(1)}, u32[]{:S(2)}, u32[]{:S(2)}) collective-permute-start(bf16[256,512]{1,0:T(8,128)(2,1)S(1)} %collective-permute-done.4), channel_id=1, source_target_pairs={{0,2},{2,4},{4,6},{6,8},{8,10},{10,12},{12,14},{14,16},{16,18},{18... | collective-permute-start | bytes 786440 | tf_op jit(solution)/shard_map/ppermute | solution.py:67
  165.2 10.9 %collective-permute-start.6 = (bf16[256,512]{1,0:T(8,128)(2,1)S(1)}, bf16[256,512]{1,0:T(8,128)(2,1)S(1)}, u32[]{:S(2)}, u32[]{:S(2)}) collective-permute-start(bf16[256,512]{1,0:T(8,128)(2,1)S(1)} %collective-permute-done.5), channel_id=1, source_target_pairs={{0,2},{2,4},{4,6},{6,8},{8,10},{10,12},{12,14},{14,16},{16,18},{18... | collective-permute-start | bytes 786440 | tf_op jit(solution)/shard_map/ppermute | solution.py:67
  176.0 10.1 %collective-permute-start.7 = (bf16[256,512]{1,0:T(8,128)(2,1)S(1)}, bf16[256,512]{1,0:T(8,128)(2,1)S(1)}, u32[]{:S(2)}, u32[]{:S(2)}) collective-permute-start(bf16[256,512]{1,0:T(8,128)(2,1)S(1)} %collective-permute-done.6), channel_id=1, source_target_pairs={{0,2},{2,4},{4,6},{6,8},{8,10},{10,12},{12,14},{14,16},{16,18},{18... | collective-permute-start | bytes 786440 | tf_op jit(solution)/shard_map/ppermute | solution.py:67
  186.1 9.2 %collective-permute-start.8 = (bf16[256,512]{1,0:T(8,128)(2,1)S(1)}, bf16[256,512]{1,0:T(8,128)(2,1)S(1)}, u32[]{:S(2)}, u32[]{:S(2)}) collective-permute-start(bf16[256,512]{1,0:T(8,128)(2,1)S(1)} %collective-permute-done.7), channel_id=1, source_target_pairs={{0,2},{2,4},{4,6},{6,8},{8,10},{10,12},{12,14},{14,16},{16,18},{18... | collective-permute-start | bytes 786440 | tf_op jit(solution)/shard_map/ppermute | solution.py:67
  203.8 9.0 collective-permute-start.10
  212.8 8.9 collective-permute-start.11
  221.7 9.1 collective-permute-start.12
  221.8 402.4 %all-reduce.7.cloned.1.call-start = ((), (), s32[]{:S(2)}) async-start(), calls=%async_computation.8 | async-start | bytes 262144 | tf_op jit(solution)/shard_map/psum | solution.py:100
  230.8 13.2 %collective-permute-start.13 = (bf16[256,512]{1,0:T(8,128)(2,1)}, bf16[256,512]{1,0:T(8,128)(2,1)}, u32[]{:S(2)}, u32[]{:S(2)}) collective-permute-start(bf16[256,512]{1,0:T(8,128)(2,1)} %collective-permute-done.12), channel_id=1, source_target_pairs={{0,2},{2,4},{4,6},{6,8},{8,10},{10,12},{12,14},{14,16},{16,18},{18... | collective-permute-start | bytes 786440 | tf_op jit(solution)/shard_map/ppermute | solution.py:67
  244.0 125.2 %collective-permute-start.14 = (bf16[256,512]{1,0:T(8,128)(2,1)}, bf16[256,512]{1,0:T(8,128)(2,1)}, u32[]{:S(2)}, u32[]{:S(2)}) collective-permute-start(bf16[256,512]{1,0:T(8,128)(2,1)} %collective-permute-done.13), channel_id=1, source_target_pairs={{0,2},{2,4},{4,6},{6,8},{8,10},{10,12},{12,14},{14,16},{16,18},{18... | collective-permute-start | bytes 786440 | tf_op jit(solution)/shard_map/ppermute | solution.py:67
  589.4 72.9 %all-reduce.9.cloned.1.call-start = ((), (), s32[]{:S(2)}) async-start(), calls=%async_computation.12 | async-start | bytes 262144 | tf_op jit(solution)/shard_map/psum | solution.py:114
  626.3 115.0 %reduce-scatter.4.cloned.1.call-start = ((), (), s32[]{:S(2)}) async-start(), calls=%async_computation.10 | async-start | bytes 2228224 | tf_op jit(solution)/shard_map/reduce_scatter | solution.py:127
  630.7 193.2 %reduce-scatter.6.cloned.1.call-start = ((), (), s32[]{:S(2)}) async-start(), calls=%async_computation.13 | async-start | bytes 2228224 | tf_op jit(solution)/shard_map/reduce_scatter | solution.py:130
  668.3 241.3 %reduce-scatter.8.cloned.1.call-start = ((), (), s32[]{:S(2)}) async-start(), calls=%async_computation.14 | async-start | bytes 4456448 | tf_op jit(solution)/shard_map/reduce_scatter | solution.py:138
  (7 other events, 481.0 us)
Sparse Core Ops, SparseCore 0:
  11.0 55.3 all-gather.9
  68.1 102.5 all-gather.11
  173.7 73.2 all-gather.17
  248.7 115.4 all-gather.15
  365.8 108.0 all-gather.13
  475.6 108.0 all-gather.7
  589.5 34.5 all-reduce.6
  627.3 34.9 all-reduce.8
  665.8 75.4 reduce-scatter.3
  745.1 78.6 reduce-scatter.5
  827.5 82.0 reduce-scatter.7
